TPU v7x, 32 devices: a whole 2x2x4 slice. The times are simulated.
32 devices in a mesh: path: 8 (over z, x), shard: 4 (over y, core).
Axes of the slice: x: 2, y: 2, z: 4, core: 2. Of those that a mesh axis runs over, the one named last changes fastest.
Arguments:
- master: float32 [2, 4096, 2048], P(None, ('path', 'shard')), may hold values from -6 to 6
- momentum: float32 [2, 4096, 2048], P(None, ('path', 'shard')), may hold values from -2 to 2
- routes: int32 [8, 1], replicated, may hold values from 0 to 1
- counts: int32 [8], replicated, may hold values from 1 to 8
- tokens: bfloat16 [12288, 4096], P(('path', 'shard')), may hold values from -6 to 6
- cotangent: bfloat16 [12288, 2048], P(('path', 'shard')), may hold values from -6 to 6
Outputs:
- master_new: float32 [2, 4096, 2048], P(None, ('path', 'shard'))
- momentum_new: float32 [2, 4096, 2048], P(None, ('path', 'shard'))
Inputs may be any that keep to these rules, and one draw needn't show every extreme that they name: `routes`: every module is read by at least one path.
All inputs are finite; a program needn't handle non-finite values.
Results may differ from a plain program's by a relative error of at most 0.0032.
Values may be sent and summed in bfloat16 or wider, within the bound.
No kernel may reach another device: no remote copies, remote signals or barrier semaphores. Data moves between devices by JAX's collectives and lax.ppermute only.
A program may use at most 128 MiB of HBM per device.

v0:
```python
import jax
import jax.numpy as jnp
from jax import lax
from jax.sharding import PartitionSpec as P


def local(master, momentum, routes, counts, tokens, cotangent):
    path_count = routes.shape[0]
    shards = lax.axis_size("shard")
    modules = master.shape[0]
    rows_block = master.shape[1]
    feat_width = master.shape[2]
    tok_rows = tokens.shape[0]
    model_width = tokens.shape[1]
    inv_root = model_width ** (-0.5)
    chosen = routes[:, 0]
    onehot = (chosen[None, :] == jnp.arange(modules, dtype=jnp.int32)[:, None]).astype(jnp.float32)
    outgoing = jnp.take(master.astype(jnp.bfloat16), chosen, axis=0)
    local_rows = lax.all_to_all(outgoing, "path", split_axis=0, concat_axis=0, tiled=True)
    local_weight = local_rows.reshape(path_count * rows_block, feat_width)
    permuted = tokens.reshape(tok_rows, path_count, shards, rows_block)
    permuted = permuted.transpose(0, 2, 1, 3).reshape(tok_rows, model_width)
    columns = lax.all_to_all(permuted, "shard", split_axis=1, concat_axis=0, tiled=True)
    columns_part = permuted
    pre_sum = jnp.dot(
        columns_part,
        lax.all_gather(local_weight, "shard", axis=0, tiled=True),
        preferred_element_type=jnp.float32,
    )
    pre_act = pre_sum * inv_root
    gate_value = jax.nn.sigmoid(pre_act)
    signal = (
        cotangent.astype(jnp.float32) * gate_value * (1.0 + pre_act * (1.0 - gate_value))
    ).astype(jnp.bfloat16)
    columns_part = columns
    product = lax.dot_general(
        columns_part,
        lax.all_gather(signal, "shard", axis=0, tiled=True),
        (((0,), (0,)), ((), ())),
        preferred_element_type=jnp.float32,
    )
    path_grad = (
        (product * inv_root).astype(jnp.bfloat16).reshape(path_count, rows_block, feat_width)
    )
    received = lax.all_to_all(path_grad, "path", split_axis=0, concat_axis=0, tiled=True)
    mixing = onehot * counts.astype(jnp.float32)[None, :]
    mixing = mixing / jnp.sum(mixing, axis=1, keepdims=True)
    flat_recv = received.reshape(path_count, rows_block * feat_width).astype(jnp.float32)
    outer_grad = jnp.dot(mixing, flat_recv, precision=lax.Precision.HIGHEST).reshape(
        modules, rows_block, feat_width
    )
    momentum_new = 0.9 * momentum + outer_grad
    master_new = master - 0.7 * (outer_grad + 0.9 * momentum_new)
    return (master_new, momentum_new)


def solution(mesh):
    placed = (
        P(None, ("path", "shard"), None),
        P(None, ("path", "shard"), None),
        P(),
        P(),
        P(("path", "shard"), None),
        P(("path", "shard"), None),
    )
    return jax.shard_map(
        local,
        mesh=mesh,
        in_specs=placed,
        out_specs=(P(None, ("path", "shard"), None), P(None, ("path", "shard"), None)),
        check_vma=False,
    )
```

profile of v0, /device:TPU:0, one launch (start us, length us, event | category | flops | bytes accessed | tf_op | source)
XLA Modules:
  0.0 444.9 jit_solution(9973681836863088704)
XLA Ops:
  7.2 0.0 all-gather.3.cloned.1.call-start
  7.2 0.7 fusion.16
  7.9 0.7 and_bitcast_fusion
  8.5 1.7 convert_element_type.22
  10.3 2.8 gather_fusion
  13.0 2.7 broadcast_select_fusion
  15.7 100.3 %all_to_all.29 = bf16[8,128,2048]{2,1,0:T(8,128)(2,1)} all-to-all(bf16[8,128,2048]{2,1,0:T(8,128)(2,1)S(1)} %broadcast_select_fusion), channel_id=1, replica_groups=mesh['path'=8,'shard'=4] {'path'}, dimensions={0} | all-to-all | bytes 8388608 | tf_op jit(solution)/shard_map/all_to_all | solution.py:19
  116.0 0.0 copy-start
  116.0 0.0 all-gather.3.cloned.1.call-update
  116.1 0.0 all-gather.5.cloned.1.call-start
  116.1 1.8 copy-done
  117.9 2.8 copy.27
  120.7 2.7 copy.28
  123.5 2.8 copy.26
  126.3 94.9 %all-gather.3.cloned.1.call-done = bf16[4096,2048]{1,0:T(8,128)(2,1)} async-done(((bf16[1024,2048]{1,0:T(8,128)(2,1)}), bf16[4096,2048]{1,0:T(8,128)(2,1)}) %all-gather.3.cloned.1.call-update) | async-done | bytes 16777232 | tf_op jit(solution)/shard_map/all_gather | solution.py:27
  221.2 14.3 %fusion.5 = bf16[384,2048]{0,1:T(8,128)(2,1)} fusion(bf16[384,2048]{0,1:T(8,128)(2,1)} %copy.26, bf16[4096,2048]{1,0:T(8,128)(2,1)} %all-gather.3.cloned.1.call-done, bf16[384,4096]{0,1:T(8,128)(2,1)S(1)} %bitcast.51), kind=kOutput, calls=%fused_computation.11 | convolution fusion | flops 6451101696 | bytes 23068672 | tf_op jit(solution)/shard_map/dot_general | solution.py:25
  235.5 0.0 all-gather.5.cloned.1.call-update
  235.5 69.7 %all_to_all.30 = bf16[384,4,1024]{0,2,1:T(8,128)(2,1)} all-to-all(bf16[384,4,1024]{0,2,1:T(8,128)(2,1)S(1)} %bitcast.52), channel_id=1, replica_groups=mesh['path'=8,'shard'=4] {'shard'}, dimensions={1} | all-to-all | bytes 6291456 | tf_op jit(solution)/shard_map/all_to_all | solution.py:23
  305.1 3.2 copy.30
  308.4 2.6 all-gather.5.cloned.1.call-done
  311.0 11.1 %multiply_convert_fusion = bf16[2048,1024]{0,1:T(8,128)(2,1)} fusion(bf16[1536,2048]{0,1:T(8,128)(2,1)} %all-gather.5.cloned.1.call-done, bf16[1536,1024]{1,0:T(8,128)(2,1)S(1)} %bitcast.56), kind=kOutput, calls=%fused_computation.1 | convolution fusion | flops 6446645248 | bytes 13631488 | tf_op jit(solution)/shard_map/dot_general | solution.py:36
  322.1 0.0 copy-start.2
  322.1 0.0 copy-start.3
  322.1 0.0 copy-start.1
  322.1 5.6 %all-to-all-start.2 = ((bf16[8,128,2048]{2,1,0:T(8,128)(2,1)}), bf16[8,128,2048]{2,1,0:T(8,128)(2,1)}, u32[]{:S(2)}, u32[]{:S(2)}) async-start(bf16[8,128,2048]{2,1,0:T(8,128)(2,1)} %bitcast.55), calls=%async_computation.2 | async-start | bytes 8388608 | tf_op jit(solution)/shard_map/all_to_all | solution.py:45
  327.8 0.0 copy-done.2
  327.8 0.0 copy-done.3
  327.8 0.1 fusion.10
  327.9 93.6 %all-to-all-done.2 = bf16[8,128,2048]{2,1,0:T(8,128)(2,1)} async-done(((bf16[8,128,2048]{2,1,0:T(8,128)(2,1)}), bf16[8,128,2048]{2,1,0:T(8,128)(2,1)}, u32[]{:S(2)}, u32[]{:S(2)}) %all-to-all-start.2) | async-done | bytes 4194336 | tf_op jit(solution)/shard_map/all_to_all | solution.py:45
  421.5 0.0 copy-done.1
  421.5 11.5 %fusion.6 = (f32[2,128,2048]{2,0,1:T(2,128)S(1)}, f32[2,128,2048]{2,0,1:T(2,128)S(1)}) fusion(f32[2,128,2048]{2,1,0:T(8,128)} %param.7, f32[2,128,2048]{2,1,0:T(8,128)S(1)} %copy-done.1, f32[2]{0:T(128)S(1)} %fusion.10, f32[8]{0:T(128)S(1)} %convert_element_type.20, s32[8]{0:T(128)S(1)} %bitcast.58, bf16[1,8,128,2048]{3,2,1,0:T(8,128)(2,1)} %bitcast.19), kind=kOutput, calls=%fused_computation.14 | convolution fusion | flops 53477424 | bytes 12582984 | tf_op jit(solution)/shard_map/dot_general | solution.py:49
  433.0 2.5 copy.33
  435.5 2.5 copy.34
  (2 shorter events, 0.0 us)
Async XLA Ops:
  7.2 214.0 %all-gather.3.cloned.1.call-start = ((), (), s32[]{:S(2)}) async-start(), calls=%async_computation.3 | async-start | bytes 20971520 | tf_op jit(solution)/shard_map/all_gather | solution.py:27
  116.0 1.9 copy-start
  116.1 194.9 %all-gather.5.cloned.1.call-start = ((), (), s32[]{:S(2)}) async-start(), calls=%async_computation.4 | async-start | bytes 7864320 | tf_op jit(solution)/shard_map/all_gather | solution.py:38
  322.1 5.7 %copy-start.2 = (s32[8]{0:T(128)S(1)}, s32[8]{0:T(128)}, u32[]{:S(2)}) copy-start(s32[8]{0:T(128)} %param.9) | copy-start | bytes 100
  322.1 5.7 %copy-start.3 = (s32[8,1]{0,1:T(1,128)S(1)}, s32[8,1]{0,1:T(1,128)}, u32[]{:S(2)}) copy-start(s32[8,1]{0,1:T(1,128)} %param.8) | copy-start | bytes 100
  322.1 99.3 %copy-start.1 = (f32[2,128,2048]{2,1,0:T(8,128)S(1)}, f32[2,128,2048]{2,1,0:T(8,128)}, u32[]{:S(2)}) copy-start(f32[2,128,2048]{2,1,0:T(8,128)} %param.6) | copy-start | bytes 6291460
  322.1 99.3 %all-to-all-start.2 = ((bf16[8,128,2048]{2,1,0:T(8,128)(2,1)}), bf16[8,128,2048]{2,1,0:T(8,128)(2,1)}, u32[]{:S(2)}, u32[]{:S(2)}) async-start(bf16[8,128,2048]{2,1,0:T(8,128)(2,1)} %bitcast.55), calls=%async_computation.2 | async-start | bytes 8388608 | tf_op jit(solution)/shard_map/all_to_all | solution.py:45
Sparse Core Ops, SparseCore 0:
  116.2 104.9 all-gather.2
  235.6 75.3 all-gather.4
where the time goes:
time: 445 us
  waiting for transfers between devices  191 us (43%)
  blocking collectives  170 us (38%)
  matrix products  36.9 us (8%)
  local copies, waits for them, and re-layouts  21.2 us (5%)
  between operations  14.1 us (3%)
  other arithmetic  5.83 us (1%)
  starting transfers between devices  5.72 us (1%)
    all_to_all x1, blocking collectives, local(): lax.all_to_all(outgoing, 'path', split_axis=0, concat_axis=0, tiled=True)  100 us
    all_gather x1, waiting for transfers between devices, local(): lax.all_gather(local_weight, 'shard', axis=0, tiled=True)  94.9 us
    all_to_all x1, waiting for transfers between devices, local(): lax.all_to_all(path_grad, 'path', split_axis=0, concat_axis=0, tiled=True)  93.6 us
    all_to_all x1, blocking collectives, local(): lax.all_to_all(permuted, 'shard', split_axis=1, concat_axis=0, tiled=True)  69.7 us
    dot_general x1, matrix products, local(): jnp.dot(columns_part, lax.all_gather(local_weight, 'shard', axis=0, tiled...  14.3 us
    unnamed x12, local copies, waits for them, and re-layouts  12.5 us
    dot_general x1, matrix products, local(): jnp.dot(mixing, flat_recv, precision=lax.Precision.HIGHEST)  11.5 us
    dot_general x1, matrix products, local(): lax.dot_general(columns_part, lax.all_gather(signal, 'shard', axis=0, til...  11.1 us
  transfers between devices with their start and end apart: 3, of which 3 were waited for; matrix products, arithmetic and copies ran while one was open for 3% of the time, Pallas kernels for 0%

commit v1 on v0

--- a/solution.py
+++ b/solution.py
@@ -20,7 +20,12 @@
     local_weight = local_rows.reshape(path_count * rows_block, feat_width)
     permuted = tokens.reshape(tok_rows, path_count, shards, rows_block)
     permuted = permuted.transpose(0, 2, 1, 3).reshape(tok_rows, model_width)
-    columns = lax.all_to_all(permuted, "shard", split_axis=1, concat_axis=0, tiled=True)
+    columns = jnp.concatenate(
+        lax.all_to_all(
+            jnp.stack(jnp.split(permuted, lax.axis_size("shard"), axis=1)), "shard", 0, 0
+        ),
+        axis=0,
+    )
     columns_part = permuted
     pre_sum = jnp.dot(
         columns_part,

time: 445 us -> 446 us (level)
  no operation moved by 1% of the time
where the time goes in v1:
time: 446 us; the launch traced here: 445 us
  waiting for transfers between devices  193 us (43%)
  blocking collectives  169 us (38%)
  matrix products  37 us (8%)
  local copies, waits for them, and re-layouts  19.4 us (4%)
  between operations  14.1 us (3%)
  other arithmetic  6.37 us (1%)
  starting transfers between devices  5.74 us (1%)
    all_to_all x1, blocking collectives, local(): lax.all_to_all(outgoing, 'path', split_axis=0, concat_axis=0, tiled=True)  100 us
    all_gather x1, waiting for transfers between devices, local(): lax.all_gather(local_weight, 'shard', axis=0, tiled=True)  96.8 us
    all_to_all x1, waiting for transfers between devices, local(): lax.all_to_all(path_grad, 'path', split_axis=0, concat_axis=0, tiled=True)  93.6 us
    all_to_all x1, blocking collectives, local(): lax.all_to_all(jnp.stack(jnp.split(permuted, lax.axis_size('shard'), axis...  69 us
    dot_general x1, matrix products, local(): jnp.dot(columns_part, lax.all_gather(local_weight, 'shard', axis=0, tiled...  14.3 us
    dot_general x1, matrix products, local(): jnp.dot(mixing, flat_recv, precision=lax.Precision.HIGHEST)  11.5 us
    dot_general x1, matrix products, local(): lax.dot_general(columns_part, lax.all_gather(signal, 'shard', axis=0, til...  11.2 us
    unnamed x12, local copies, waits for them, and re-layouts  10.6 us
  transfers between devices with their start and end apart: 3, of which 3 were waited for; matrix products, arithmetic and copies ran while one was open for 3% of the time, Pallas kernels for 0%

profile of v1, /device:TPU:0, one launch (start us, length us, event | category | flops | bytes accessed | tf_op | source)
XLA Modules:
  0.0 445.1 jit_solution(12896222260024950243)
XLA Ops:
  7.2 0.0 all-gather.3.cloned.1.call-start
  7.2 0.7 and_bitcast_fusion
  7.9 0.7 fusion.16
  8.5 1.7 convert_element_type.19
  10.3 2.8 gather_fusion
  13.0 2.7 broadcast_select_fusion
  15.7 100.3 %all_to_all.15 = bf16[8,128,2048]{2,1,0:T(8,128)(2,1)} all-to-all(bf16[8,128,2048]{2,1,0:T(8,128)(2,1)S(1)} %broadcast_select_fusion), channel_id=1, replica_groups=mesh['path'=8,'shard'=4] {'path'}, dimensions={0} | all-to-all | bytes 8388608 | tf_op jit(solution)/shard_map/all_to_all | solution.py:19
  116.0 0.0 copy-start
  116.0 0.0 all-gather.3.cloned.1.call-update
  116.1 0.0 all-gather.5.cloned.1.call-start
  116.1 2.7 copy.21
  118.9 0.0 copy-done
  118.9 2.8 copy.18
  121.6 2.7 copy.19
  124.4 96.8 %all-gather.3.cloned.1.call-done = bf16[4096,2048]{1,0:T(8,128)(2,1)} async-done(((bf16[1024,2048]{1,0:T(8,128)(2,1)}), bf16[4096,2048]{1,0:T(8,128)(2,1)}) %all-gather.3.cloned.1.call-update) | async-done | bytes 16777232 | tf_op jit(solution)/shard_map/all_gather | solution.py:32
  221.2 14.3 %fusion.5 = bf16[384,2048]{0,1:T(8,128)(2,1)} fusion(bf16[384,2048]{0,1:T(8,128)(2,1)} %copy.21, bf16[4096,2048]{1,0:T(8,128)(2,1)} %all-gather.3.cloned.1.call-done, bf16[384,4096]{0,1:T(8,128)(2,1)S(1)} %bitcast.55), kind=kOutput, calls=%fused_computation.12 | convolution fusion | flops 6451101696 | bytes 23068672 | tf_op jit(solution)/shard_map/dot_general | solution.py:30
  235.5 0.0 all-gather.5.cloned.1.call-update
  235.5 0.3 slice_bitcast_fusion.3
  235.8 0.5 pad_maximum_fusion
  236.4 69.0 %all_to_all.16 = bf16[4,384,1024]{1,2,0:T(8,128)(2,1)S(1)} all-to-all(bf16[4,384,1024]{1,2,0:T(8,128)(2,1)S(1)} %pad_maximum_fusion), channel_id=1, replica_groups=mesh['path'=8,'shard'=4] {'shard'}, dimensions={0} | all-to-all | bytes 6291456 | tf_op jit(solution)/shard_map/all_to_all | solution.py:24
  305.3 2.9 copy.20
  308.3 2.9 all-gather.5.cloned.1.call-done
  311.1 11.2 %multiply_convert_fusion = bf16[1024,2048]{1,0:T(8,128)(2,1)} fusion(bf16[1536,1024]{1,0:T(8,128)(2,1)} %bitcast.59, bf16[1536,2048]{0,1:T(8,128)(2,1)} %all-gather.5.cloned.1.call-done), kind=kOutput, calls=%fused_computation.1 | convolution fusion | flops 6446645248 | bytes 13631488 | tf_op jit(solution)/shard_map/dot_general | solution.py:41
  322.3 0.0 copy-start.2
  322.3 0.0 copy-start.3
  322.3 0.0 copy-start.1
  322.3 5.7 %all-to-all-start.2 = ((bf16[8,128,2048]{2,1,0:T(8,128)(2,1)}), bf16[8,128,2048]{2,1,0:T(8,128)(2,1)}, u32[]{:S(2)}, u32[]{:S(2)}) async-start(bf16[8,128,2048]{2,1,0:T(8,128)(2,1)} %bitcast.58), calls=%async_computation.2 | async-start | bytes 8388608 | tf_op jit(solution)/shard_map/all_to_all | solution.py:50
  328.0 0.0 copy-done.2
  328.0 0.0 copy-done.3
  328.0 0.1 fusion.10
  328.1 93.6 %all-to-all-done.2 = bf16[8,128,2048]{2,1,0:T(8,128)(2,1)} async-done(((bf16[8,128,2048]{2,1,0:T(8,128)(2,1)}), bf16[8,128,2048]{2,1,0:T(8,128)(2,1)}, u32[]{:S(2)}, u32[]{:S(2)}) %all-to-all-start.2) | async-done | bytes 4194336 | tf_op jit(solution)/shard_map/all_to_all | solution.py:50
  421.7 0.0 copy-done.1
  421.7 11.5 %fusion.6 = (f32[2,128,2048]{2,0,1:T(2,128)S(1)}, f32[2,128,2048]{2,0,1:T(2,128)S(1)}) fusion(f32[2,128,2048]{2,1,0:T(8,128)} %param.7, f32[2,128,2048]{2,1,0:T(8,128)S(1)} %copy-done.1, f32[2]{0:T(128)S(1)} %fusion.10, f32[8]{0:T(128)S(1)} %convert_element_type.17, s32[8]{0:T(128)S(1)} %bitcast.61, bf16[1,8,128,2048]{3,2,1,0:T(8,128)(2,1)} %bitcast.19), kind=kOutput, calls=%fused_computation.15 | convolution fusion | flops 53477424 | bytes 12582984 | tf_op jit(solution)/shard_map/dot_general | solution.py:54
  433.2 2.5 copy.25
  435.7 2.5 copy.24
  (2 shorter events, 0.0 us)
Async XLA Ops:
  7.2 214.0 %all-gather.3.cloned.1.call-start = ((), (), s32[]{:S(2)}) async-start(), calls=%async_computation.3 | async-start | bytes 20971520 | tf_op jit(solution)/shard_map/all_gather | solution.py:32
  116.0 2.8 copy-start
  116.1 195.0 %all-gather.5.cloned.1.call-start = ((), (), s32[]{:S(2)}) async-start(), calls=%async_computation.4 | async-start | bytes 7864320 | tf_op jit(solution)/shard_map/all_gather | solution.py:43
  322.3 5.7 %copy-start.2 = (s32[8]{0:T(128)S(1)}, s32[8]{0:T(128)}, u32[]{:S(2)}) copy-start(s32[8]{0:T(128)} %param.9) | copy-start | bytes 100
  322.3 5.7 %copy-start.3 = (s32[8,1]{0,1:T(1,128)S(1)}, s32[8,1]{0,1:T(1,128)}, u32[]{:S(2)}) copy-start(s32[8,1]{0,1:T(1,128)} %param.8) | copy-start | bytes 100
  322.3 99.4 %copy-start.1 = (f32[2,128,2048]{2,1,0:T(8,128)S(1)}, f32[2,128,2048]{2,1,0:T(8,128)}, u32[]{:S(2)}) copy-start(f32[2,128,2048]{2,1,0:T(8,128)} %param.6) | copy-start | bytes 6291460
  322.3 99.4 %all-to-all-start.2 = ((bf16[8,128,2048]{2,1,0:T(8,128)(2,1)}), bf16[8,128,2048]{2,1,0:T(8,128)(2,1)}, u32[]{:S(2)}, u32[]{:S(2)}) async-start(bf16[8,128,2048]{2,1,0:T(8,128)(2,1)} %bitcast.58), calls=%async_computation.2 | async-start | bytes 8388608 | tf_op jit(solution)/shard_map/all_to_all | solution.py:50
Sparse Core Ops, SparseCore 0:
  116.2 104.9 all-gather.2
  235.6 75.4 all-gather.4
